TPU v7x, 256 devices: a whole 4x4x8 slice. The times are simulated.
256 devices in a mesh: chan: 64 (over z_hi, x, y, core), tm: 4 (over z_lo).
Axes of the slice: x: 4, y: 4, z: 8 (z_hi: 2, z_lo: 4; z = z_hi * 4 + z_lo), core: 2. Of those that a mesh axis runs over, the one named last changes fastest.
Arguments:
- spectra: bfloat16 [64, 8, 2, 6144], P(None, 'tm', None, 'chan'), may hold values from -120 to 120
- bad_channels: int32 [6144], P('chan'), may hold values 0 or 1
- tile_list: int32 [512, 2], P('chan'), may hold values from 0 to 47, as said below
Outputs:
- correlations: float32 [512, 32, 128, 128], P(('chan', 'tm'))
Inputs may be any that keep to these rules, and one draw needn't show every extreme that they name: `tile_list`: each row (a, b) has a <= b; a pair may appear more than once.
All inputs are finite; a program needn't handle non-finite values. No bound on the sum of `bad_channels` on one device may be relied on, other than what follows from the above.
Results may differ from a plain program's by a relative error of at most 0.004.
Values may be sent and summed in bfloat16 or wider, within the bound.
A program may use at most 128 MiB of HBM per device.

v0:
```python
import math
import jax
import jax.numpy as jnp
from jax import lax
from jax.sharding import PartitionSpec as P

HR_DEV = 2
F = 64
LAGS = 32
TILE = 128
EPSILON = 1e-06


def whiten(spectra, bad_channels):
    values = spectra.astype(jnp.float32)
    power = jnp.mean(values * values, axis=(0, 2))
    keep_mask = (1 - bad_channels).astype(jnp.float32)
    white = values * lax.rsqrt(power + EPSILON)[None, :, None, :] * keep_mask[None, None, None, :]
    return white.astype(jnp.bfloat16)


def lag_table(hour_count):
    bin_number = jnp.arange(F, dtype=jnp.float32) + 1.0
    lag_steps = jnp.arange(LAGS, dtype=jnp.float32) - float(LAGS // 2)
    phases = math.pi / F * bin_number[:, None] * lag_steps[None, :]
    norm_scale = 1.0 / math.sqrt(F * hour_count)
    return jnp.stack([jnp.cos(phases) * norm_scale, -jnp.sin(phases) * norm_scale], axis=1)


def take_block(spectra_all, block_index):
    return lax.dynamic_slice_in_dim(spectra_all, block_index * TILE, TILE, axis=3)


def cross_spec(spectra_all, tile_pair):
    left_block = take_block(spectra_all, tile_pair[0])
    right_block = take_block(spectra_all, tile_pair[1])
    bin_total = left_block.shape[0]
    hour_count = left_block.shape[1]
    row_block = left_block.reshape(bin_total, 2 * hour_count, TILE)
    turned = jnp.stack([-right_block[:, :, 1], right_block[:, :, 0]], axis=2)
    col_block = jnp.concatenate([right_block, turned], axis=3).reshape(
        bin_total, 2 * hour_count, 2 * TILE
    )
    return jnp.einsum("fki,fkj->fij", row_block, col_block, preferred_element_type=jnp.float32)


def transform(cross, table):
    parted = cross.reshape(cross.shape[0], TILE, 2, TILE)
    return jnp.einsum("fixj,fxt->tij", parted, table, precision=lax.Precision.HIGHEST)


def tile_lags(spectra_all, table, pairs):
    return jax.vmap(lambda tile_pair: transform(cross_spec(spectra_all, tile_pair), table))(pairs)


def per_device(spectra, bad_channels, tile_list):
    white = whiten(spectra, bad_channels)
    tile_dev = tile_list.shape[0] // lax.axis_size("tm")
    table = lag_table(HR_DEV * lax.axis_size("tm"))
    hours_all = lax.all_gather(white, "tm", axis=1, tiled=True)
    spectra_all = lax.all_gather(hours_all, "chan", axis=3, tiled=True)
    own_pairs = lax.dynamic_slice_in_dim(
        tile_list, lax.axis_index("tm") * tile_dev, tile_dev, axis=0
    )
    return tile_lags(spectra_all, table, own_pairs)


def solution(mesh):
    placed = (P(None, "tm", None, "chan"), P("chan"), P("chan", None))
    return jax.shard_map(
        per_device,
        mesh=mesh,
        in_specs=placed,
        out_specs=P(("chan", "tm"), None, None, None),
        check_vma=False,
    )
```

profile of v0, /device:TPU:1, one launch (start us, length us, event | category | flops | bytes accessed | tf_op | source)
XLA Modules:
  0.0 306.1 jit_solution(9711034003275333782)
XLA Ops:
  6.5 0.0 copy-start
  6.5 0.0 all-gather.2.cloned.1.call-start
  6.5 0.9 fusion.7
  7.4 0.7 subtract_convert_fusion
  8.1 0.9 fusion.9
  9.0 13.7 %all_gather.6 = bf16[64,8,2,96]{3,0,2,1:T(8,128)(2,1)S(1)} all-gather(bf16[64,2,2,96]{3,0,2,1:T(8,128)(2,1)S(1)} %fusion.9), channel_id=1, replica_groups=mesh['chan'=64,'tm'=4] {'tm'}, dimensions={1}, use_global_device_ids=true | all-gather | bytes 245760 | tf_op jit(solution)/shard_map/all_gather | solution.py:60
  22.7 1.1 copy.15
  23.7 0.0 all-gather.2.cloned.1.call-update
  23.8 0.0 copy-done
  23.8 0.1 constant_dynamic-slice_fusion
  23.9 0.1 fusion.12
  24.0 204.5 %all-gather.2.cloned.1.call-done = bf16[64,8,2,6144]{0,1,2,3:T(8,128)(2,1)} async-done(((bf16[64,8,2,96]{0,1,2,3:T(8,128)(2,1)}), bf16[64,8,2,6144]{0,1,2,3:T(8,128)(2,1)}) %all-gather.2.cloned.1.call-update) | async-done | bytes 12582928 | tf_op jit(solution)/shard_map/all_gather | solution.py:61
  228.5 8.9 %gather_fusion.1 = bf16[2,64,8,2,128]{1,2,3,4,0:T(8,128)(2,1)S(1)} fusion(bf16[64,8,2,6144]{0,1,2,3:T(8,128)(2,1)} %all-gather.2.cloned.1.call-done, s32[2]{0:T(128)S(1)} %get-tuple-element.10), kind=kCustom, calls=%fused_computation.1 | custom fusion | bytes 1048608 | tf_op jit(solution)/shard_map/vmap()/gather | solution.py:31
  237.4 0.1 slice_negate_fusion
  237.6 0.5 maximum_maximum_fusion
  238.1 3.1 %copy.17 = bf16[2,64,8,2,256]{4,3,2,1,0:T(2,128)(2,1)S(1)} copy(bf16[2,64,8,2,256]{1,2,3,4,0:T(8,128)(2,1)S(1)} %maximum_maximum_fusion) | data formatting | bytes 2097152 | tf_op jit(solution)/shard_map/vmap()/concatenate | solution.py:41
  241.2 0.4 reshape.116
  241.6 8.9 %gather_fusion = bf16[2,64,8,2,128]{1,2,3,4,0:T(8,128)(2,1)S(1)} fusion(bf16[64,8,2,6144]{0,1,2,3:T(8,128)(2,1)} %all-gather.2.cloned.1.call-done, s32[2]{0:T(128)S(1)} %get-tuple-element.9), kind=kCustom, calls=%fused_computation | custom fusion | bytes 1048608 | tf_op jit(solution)/shard_map/vmap()/gather | solution.py:31
  250.5 0.9 copy.16
  251.4 8.1 %fusion.5 = f32[2,64,128,256]{3,2,1,0:T(8,128)} fusion(bf16[2,64,16,256]{3,2,1,0:T(8,128)(2,1)S(1)} %reshape.116, bf16[2,64,16,128]{3,1,2,0:T(8,128)(2,1)S(1)} %bitcast.18), kind=kOutput, calls=%fused_computation.7 | convolution fusion | flops 134217728 | bytes 18350080 | tf_op jit(solution)/shard_map/vmap(fki,fkj->fij)/dot_general | solution.py:44
  259.5 0.0 copy-start.1
  259.5 20.8 %reshape.117 = f32[2,64,128,2,128]{4,3,2,1,0:T(2,128)} reshape(f32[2,64,128,256]{3,2,1,0:T(8,128)} %fusion.5) | data formatting | bytes 33554432 | tf_op jit(solution)/shard_map/vmap()/reshape | solution.py:48
  280.3 14.5 %fusion.2 = f32[2,32,128,128]{3,1,2,0:T(8,128)S(1)} fusion(f32[2,64,128,2,128]{4,3,2,1,0:T(2,128)} %reshape.117, f32[64,1,32]{0,2,1:T(8,128)S(1)} %get-tuple-element.8, f32[64,1,32]{0,2,1:T(8,128)S(1)} %get-tuple-element.7), kind=kOutput, calls=%fused_computation.4 | convolution fusion | flops 1610616832 | bytes 20987904 | tf_op jit(solution)/shard_map/vmap(fixj,fxt->tij)/dot_general | solution.py:49
  294.8 4.4 %copy.20 = f32[2,32,128,128]{3,2,1,0:T(8,128)} copy(f32[2,32,128,128]{3,1,2,0:T(8,128)S(1)} %fusion.2) | data formatting | bytes 8388608 | tf_op jit(solution)/shard_map/vmap()/transpose | solution.py:53
  299.2 0.0 copy-done.1
  (4 shorter events, 0.0 us)
Async XLA Ops:
  6.5 17.3 %copy-start = (s32[8,2]{0,1:T(2,128)S(1)}, s32[8,2]{0,1:T(2,128)}, u32[]{:S(2)}) copy-start(s32[8,2]{0,1:T(2,128)} %param.5) | copy-start | bytes 196
  6.5 222.0 %all-gather.2.cloned.1.call-start = ((), (), s32[]{:S(2)}) async-start(), calls=%async_computation | async-start | bytes 25559040 | tf_op jit(solution)/shard_map/all_gather | solution.py:61
  259.5 39.7 %copy-start.1 = (s32[8,2]{0,1:T(2,128)S(1)}, s32[8,2]{0,1:T(2,128)}, u32[]{:S(2)}) copy-start(s32[8,2]{0,1:T(2,128)} %param.5) | copy-start | bytes 196
Sparse Core Ops, SparseCore 0:
  23.9 204.5 all-gather.1
where the time goes:
time: 307 us; the launch traced here: 306 us
  waiting for transfers between devices  205 us (67%)
  local copies, waits for them, and re-layouts  48.6 us (16%)
  matrix products  22.6 us (7%)
  blocking collectives  13.7 us (4%)
  between operations  13.5 us (4%)
  other arithmetic  3.19 us (1%)
    all_gather x1, waiting for transfers between devices, per_device(): spectra_all = lax.all_gather(hours_all, 'chan', axis=3, tiled=True)  204 us
    reshape x1, local copies, waits for them, and re-layouts, transform(): parted = cross.reshape(cross.shape[0], TILE, 2, TILE)  20.8 us
    gather x3, local copies, waits for them, and re-layouts, take_block(): lax.dynamic_slice_in_dim(spectra_all, block_index * TILE, TILE, axis=3)  18.7 us
    dot_general x1, matrix products, transform(): jnp.einsum('fixj,fxt->tij', parted, table, precision=lax.Precision.HIGHEST)  14.5 us
    all_gather x1, blocking collectives, per_device(): hours_all = lax.all_gather(white, 'tm', axis=1, tiled=True)  13.7 us
    dot_general x1, matrix products, cross_spec(): jnp.einsum('fki,fkj->fij', row_block, col_block, preferred_element_type=j...  8.11 us
  transfers between devices with their start and end apart: 1, of which 1 were waited for; matrix products, arithmetic and copies ran while one was open for 0% of the time, Pallas kernels for 0%

commit v1 on v0

--- a/solution.py
+++ b/solution.py
@@ -58,7 +58,11 @@
     tile_dev = tile_list.shape[0] // lax.axis_size("tm")
     table = lag_table(HR_DEV * lax.axis_size("tm"))
     hours_all = lax.all_gather(white, "tm", axis=1, tiled=True)
-    spectra_all = lax.all_gather(hours_all, "chan", axis=3, tiled=True)
+    _answer_limits = lambda own_rows, across: jnp.concatenate(
+        lax.all_to_all(jnp.stack([own_rows for _ in range(lax.axis_size(across))]), across, 0, 0),
+        axis=3,
+    )
+    spectra_all = _answer_limits(hours_all, "chan")
     own_pairs = lax.dynamic_slice_in_dim(
         tile_list, lax.axis_index("tm") * tile_dev, tile_dev, axis=0
     )

time: 307 us -> 536 us (1.75)
  waiting for transfers between devices: 205 us -> 385 us
  local copies, waits for them, and re-layouts: 48.6 us -> 91.3 us
  starting transfers between devices: 0.01 us -> 14.4 us
  between operations: 13.5 us -> 0.11 us
    all_to_all x0 -> x1, waiting for transfers between devices: none -> 385 us  [per_device(): lax.all_to_all(jnp.stack([own_rows for _ in range(lax.axis_size(across))]...]
    all_gather x1 -> x0, waiting for transfers between devices: 204 us -> none  [per_device(): spectra_all = lax.all_gather(hours_all, 'chan', axis=3, tiled=True)]
    reshape x0 -> x1, local copies, waits for them, and re-layouts: none -> 37.4 us  [per_device(): jnp.concatenate(lax.all_to_all(jnp.stack([own_rows for _ in range(lax.axi...]
    all_to_all x0 -> x1, starting transfers between devices: none -> 14.4 us  [per_device(): lax.all_to_all(jnp.stack([own_rows for _ in range(lax.axis_size(across))]...]
    another operation x0 -> x1, local copies, waits for them, and re-layouts: none -> 6.28 us  [per_device(): jnp.stack([own_rows for _ in range(lax.axis_size(across))])]
where the time goes in v1:
time: 536 us; the launch traced here: 530 us
  waiting for transfers between devices  385 us (72%)
  local copies, waits for them, and re-layouts  91.3 us (17%)
  matrix products  22.7 us (4%)
  starting transfers between devices  14.4 us (3%)
  blocking collectives  13.3 us (2%)
    all_to_all x1, waiting for transfers between devices, per_device(): lax.all_to_all(jnp.stack([own_rows for _ in range(lax.axis_size(across))]...  385 us
    reshape x1, local copies, waits for them, and re-layouts, per_device(): jnp.concatenate(lax.all_to_all(jnp.stack([own_rows for _ in range(lax.axi...  37.4 us
    reshape x1, local copies, waits for them, and re-layouts, transform(): parted = cross.reshape(cross.shape[0], TILE, 2, TILE)  20.8 us
    gather x3, local copies, waits for them, and re-layouts, take_block(): lax.dynamic_slice_in_dim(spectra_all, block_index * TILE, TILE, axis=3)  18.7 us
    dot_general x1, matrix products, transform(): jnp.einsum('fixj,fxt->tij', parted, table, precision=lax.Precision.HIGHEST)  14.6 us
    all_to_all x1, starting transfers between devices, per_device(): lax.all_to_all(jnp.stack([own_rows for _ in range(lax.axis_size(across))]...  14.4 us
    all_gather x1, blocking collectives, per_device(): hours_all = lax.all_gather(white, 'tm', axis=1, tiled=True)  13.3 us
  transfers between devices with their start and end apart: 1, of which 1 were waited for; matrix products, arithmetic and copies ran while one was open for 0% of the time, Pallas kernels for 0%

profile of v1, /device:TPU:1, one launch (start us, length us, event | category | flops | bytes accessed | tf_op | source)
XLA Modules:
  0.0 530.3 jit_solution(6958903352883062216)
XLA Ops:
  0.0 0.0 copy-start
  0.0 0.7 subtract_convert_fusion
  0.7 1.0 fusion.7
  1.6 0.9 fusion.9
  2.6 13.3 %all_gather.3 = bf16[64,8,2,96]{3,2,1,0:T(2,128)(2,1)S(1)} all-gather(bf16[64,2,2,96]{3,2,1,0:T(2,128)(2,1)S(1)} %fusion.9), channel_id=1, replica_groups=mesh['chan'=64,'tm'=4] {'tm'}, dimensions={1}, use_global_device_ids=true | all-gather | bytes 245760 | tf_op jit(solution)/shard_map/all_gather | solution.py:60
  15.9 6.3 %stack.7 = bf16[64,64,8,2,96]{4,2,3,1,0:T(8,128)(2,1)} broadcast(bf16[64,8,2,96]{3,1,2,0:T(8,128)(2,1)S(1)} %copy.14), dimensions={1,2,3,4} | broadcast | bytes 12779520 | tf_op jit(solution)/shard_map/stack | solution.py:62
  22.2 14.4 %all-to-all-start = ((bf16[64,64,8,2,96]{4,2,3,1,0:T(8,128)(2,1)}), bf16[64,64,8,2,96]{4,2,3,1,0:T(8,128)(2,1)}, u32[]{:S(2)}, u32[]{:S(2)}) async-start(bf16[64,64,8,2,96]{4,2,3,1,0:T(8,128)(2,1)} %stack.7), calls=%async_computation | async-start | bytes 33554432 | tf_op jit(solution)/shard_map/all_to_all | solution.py:62
  36.7 0.0 copy-done
  36.7 0.1 constant_dynamic-slice_fusion
  36.8 0.1 fusion.12
  36.9 385.1 %all-to-all-done = bf16[64,64,8,2,96]{4,2,3,1,0:T(8,128)(2,1)} async-done(((bf16[64,64,8,2,96]{4,2,3,1,0:T(8,128)(2,1)}), bf16[64,64,8,2,96]{4,2,3,1,0:T(8,128)(2,1)}, u32[]{:S(2)}, u32[]{:S(2)}) %all-to-all-start) | async-done | bytes 12582944 | tf_op jit(solution)/shard_map/all_to_all | solution.py:62
  422.0 37.4 %copy.15 = bf16[64,8,2,64,96]{0,1,2,4,3:T(8,128)(2,1)} copy(bf16[64,8,2,64,96]{4,1,2,0,3:T(8,128)(2,1)} %bitcast.2) | data formatting | bytes 25165824 | tf_op jit(solution)/shard_map/reshape | solution.py:61
  459.4 8.9 %gather_fusion.1 = bf16[2,64,8,2,128]{1,2,3,4,0:T(8,128)(2,1)S(1)} fusion(bf16[64,8,2,6144]{0,1,2,3:T(8,128)(2,1)} %bitcast.20, s32[2]{0:T(128)S(1)} %get-tuple-element.10), kind=kCustom, calls=%fused_computation.1 | custom fusion | bytes 1048608 | tf_op jit(solution)/shard_map/vmap()/gather | solution.py:31
  468.3 0.1 slice_negate_fusion
  468.5 0.5 maximum_maximum_fusion
  469.0 3.1 copy.17
  472.1 0.4 reshape.126
  472.5 8.9 %gather_fusion = bf16[2,64,8,2,128]{1,2,3,4,0:T(8,128)(2,1)S(1)} fusion(bf16[64,8,2,6144]{0,1,2,3:T(8,128)(2,1)} %bitcast.21, s32[2]{0:T(128)S(1)} %get-tuple-element.9), kind=kCustom, calls=%fused_computation | custom fusion | bytes 1048608 | tf_op jit(solution)/shard_map/vmap()/gather | solution.py:31
  481.4 0.9 copy.16
  482.3 8.1 %fusion.5 = f32[2,64,128,256]{3,2,1,0:T(8,128)} fusion(bf16[2,64,16,256]{3,2,1,0:T(8,128)(2,1)S(1)} %reshape.126, bf16[2,64,16,128]{3,1,2,0:T(8,128)(2,1)S(1)} %bitcast.22), kind=kOutput, calls=%fused_computation.7 | convolution fusion | flops 134217728 | bytes 18350080 | tf_op jit(solution)/shard_map/vmap(fki,fkj->fij)/dot_general | solution.py:44
  490.4 0.0 copy-start.1
  490.4 20.8 %reshape.127 = f32[2,64,128,2,128]{4,3,2,1,0:T(2,128)} reshape(f32[2,64,128,256]{3,2,1,0:T(8,128)} %fusion.5) | data formatting | bytes 33554432 | tf_op jit(solution)/shard_map/vmap()/reshape | solution.py:48
  511.2 14.6 %fusion.2 = f32[2,32,128,128]{3,1,2,0:T(8,128)S(1)} fusion(f32[2,64,128,2,128]{4,3,2,1,0:T(2,128)} %reshape.127, f32[64,1,32]{0,2,1:T(8,128)S(1)} %get-tuple-element.8, f32[64,1,32]{0,2,1:T(8,128)S(1)} %get-tuple-element.7), kind=kOutput, calls=%fused_computation.4 | convolution fusion | flops 1610616832 | bytes 20987904 | tf_op jit(solution)/shard_map/vmap(fixj,fxt->tij)/dot_general | solution.py:49
  525.9 4.4 copy.20
  530.3 0.0 copy-done.1
  (5 shorter events, 0.1 us)
Async XLA Ops:
  0.0 36.7 %copy-start = (s32[8,2]{0,1:T(2,128)S(1)}, s32[8,2]{0,1:T(2,128)}, u32[]{:S(2)}) copy-start(s32[8,2]{0,1:T(2,128)} %param.5) | copy-start | bytes 196
  22.2 399.8 %all-to-all-start = ((bf16[64,64,8,2,96]{4,2,3,1,0:T(8,128)(2,1)}), bf16[64,64,8,2,96]{4,2,3,1,0:T(8,128)(2,1)}, u32[]{:S(2)}, u32[]{:S(2)}) async-start(bf16[64,64,8,2,96]{4,2,3,1,0:T(8,128)(2,1)} %stack.7), calls=%async_computation | async-start | bytes 33554432 | tf_op jit(solution)/shard_map/all_to_all | solution.py:62
  490.4 39.9 %copy-start.1 = (s32[8,2]{0,1:T(2,128)S(1)}, s32[8,2]{0,1:T(2,128)}, u32[]{:S(2)}) copy-start(s32[8,2]{0,1:T(2,128)} %param.5) | copy-start | bytes 196
